TPU v7x, 32 devices: a whole 2x2x4 slice. The times are simulated.
32 devices in a mesh: row: 4 (over x, core), col: 4 (over z), depth: 2 (over y).
Axes of the slice: x: 2, y: 2, z: 4, core: 2. Of those that a mesh axis runs over, the one named last changes fastest.
Arguments:
- candidates: bfloat16 [4096, 512], P('row', ('col', 'depth')), may hold values from -6 to 6
- references: bfloat16 [16384, 512], P(('col', 'depth'), 'row'), may hold values from -6 to 6
- rates: float32 [16384], P(('col', 'depth')), may hold values from 0.15 to 1.5
Outputs:
- kernel: float32 [4096, 16384], P('row', ('col', 'depth'))
All inputs are finite; a program needn't handle non-finite values.
Results may differ from a plain program's by a relative error of at most 0.0003.
Values may be sent and summed in bfloat16 or wider, within the bound.
No kernel may reach another device: no remote copies, remote signals or barrier semaphores. Data moves between devices by JAX's collectives and lax.ppermute only.
A program may use at most 64 MiB of HBM per device.

v0:
```python
import jax
import jax.numpy as jnp
from jax import lax
from jax.sharding import PartitionSpec as P


def per_device(candidates, references, rates):
    paired = lax.all_gather(candidates, "depth", axis=1, tiled=True)
    panel = lax.all_gather(paired, "col", axis=1, tiled=True)
    width = panel.shape[1]
    cand_sq = jnp.sum(jnp.square(panel.astype(jnp.float32)), axis=1)
    ref_whole = lax.all_gather(references, "row", axis=1, tiled=True)
    gram = lax.dot_general(
        panel, ref_whole, (((1,), (1,)), ((), ())), preferred_element_type=jnp.float32
    )
    ref_sq = jnp.sum(jnp.square(ref_whole.astype(jnp.float32)), axis=1)
    distance = cand_sq[:, None] + ref_sq[None, :] - 2.0 * gram
    return jnp.exp(-rates[None, :] * distance / width)


def solution(mesh):
    placed = (P("row", ("col", "depth")), P(("col", "depth"), "row"), P(("col", "depth")))
    return jax.shard_map(
        per_device,
        mesh=mesh,
        in_specs=placed,
        out_specs=P("row", ("col", "depth")),
        check_vma=False,
    )
```

profile of v0, /device:TPU:0, one launch (start us, length us, event | category | flops | bytes accessed | tf_op | source)
XLA Modules:
  0.0 86.2 jit_solution(17966104002795301806)
XLA Ops:
  6.5 0.0 all-gather.3.cloned.1.call-start
  6.5 9.0 %all_gather.9 = bf16[1024,128]{0,1:T(8,128)(2,1)} all-gather(bf16[1024,64]{0,1:T(8,128)(2,1)} %param.3), channel_id=1, replica_groups=mesh['row'=4,'col'=4,'depth'=2] {'depth'}, dimensions={1}, use_global_device_ids=true | all-gather | bytes 393216 | tf_op jit(solution)/shard_map/all_gather | solution.py:8
  15.5 0.0 all-gather.3.cloned.1.call-update
  15.5 0.0 all-gather.5.cloned.1.call-start
  15.6 0.7 all-gather.5.cloned.1.call-update
  16.3 0.7 neg.4
  17.0 26.9 %all-gather.3.cloned.1.call-done = bf16[1024,512]{0,1:T(8,128)(2,1)} async-done(((bf16[1024,128]{0,1:T(8,128)(2,1)}), bf16[1024,512]{0,1:T(8,128)(2,1)}) %all-gather.3.cloned.1.call-update) | async-done | bytes 1048592 | tf_op jit(solution)/shard_map/all_gather | solution.py:9
  43.9 1.5 %multiply_reduce_fusion.1 = f32[1024]{0:T(1024)S(1)} fusion(bf16[1024,512]{0,1:T(8,128)(2,1)} %all-gather.3.cloned.1.call-done), kind=kLoop, calls=%fused_computation.2 | loop fusion | flops 1571840 | bytes 1052672 | tf_op jit(solution)/shard_map/reduce_sum | solution.py:11
  45.4 22.4 %all-gather.5.cloned.1.call-done = bf16[2048,512]{1,0:T(8,128)(2,1)} async-done(((bf16[2048,128]{1,0:T(8,128)(2,1)}), bf16[2048,512]{1,0:T(8,128)(2,1)}) %all-gather.5.cloned.1.call-update) | async-done | bytes 2097168 | tf_op jit(solution)/shard_map/all_gather | solution.py:12
  67.8 2.1 %multiply_reduce_fusion = f32[2048]{0:T(1024)S(1)} fusion(bf16[2048,512]{1,0:T(8,128)(2,1)} %all-gather.5.cloned.1.call-done), kind=kLoop, calls=%fused_computation.1 | loop fusion | flops 3143680 | bytes 2105344 | tf_op jit(solution)/shard_map/reduce_sum | solution.py:16
  69.9 9.5 %multiply_exponential_fusion = f32[1024,2048]{1,0:T(8,128)} fusion(bf16[1024,512]{0,1:T(8,128)(2,1)} %all-gather.3.cloned.1.call-done, bf16[2048,512]{1,0:T(8,128)(2,1)} %all-gather.5.cloned.1.call-done, f32[2048]{0:T(1024)S(1)} %multiply_reduce_fusion, f32[1024]{0:T(1024)S(1)} %multiply_reduce_fusion.1, f32[2048]{0:T(1024)S(1)} %neg.4), kind=kOutput, calls=%fused_computation | convolution fusion | flops 2157969408 | bytes 11554816 | tf_op jit(solution)/shard_map/dot_general | solution.py:13
Async XLA Ops:
  6.5 37.4 %all-gather.3.cloned.1.call-start = ((), (), s32[]{:S(2)}) async-start(), calls=%async_computation | async-start | bytes 1310720 | tf_op jit(solution)/shard_map/all_gather | solution.py:9
  15.5 52.3 %all-gather.5.cloned.1.call-start = ((), (), s32[]{:S(2)}) async-start(), calls=%async_computation.1 | async-start | bytes 2621440 | tf_op jit(solution)/shard_map/all_gather | solution.py:12
Sparse Core Ops, SparseCore 0:
  15.7 28.2 all-gather.2
  45.5 22.3 all-gather.4
where the time goes:
time: 86.5 us; the launch traced here: 86.2 us
  waiting for transfers between devices  50.1 us (58%)
  between operations  13.4 us (15%)
  matrix products  9.5 us (11%)
  blocking collectives  8.97 us (10%)
  other arithmetic  4.24 us (5%)
    all_gather x1, waiting for transfers between devices, per_device(): panel = lax.all_gather(paired, 'col', axis=1, tiled=True)  26.9 us
    all_gather x1, waiting for transfers between devices, per_device(): ref_whole = lax.all_gather(references, 'row', axis=1, tiled=True)  22.4 us
    dot_general x1, matrix products, per_device(): lax.dot_general(panel, ref_whole, (((1,), (1,)), ((), ())), preferred_ele...  9.5 us
    all_gather x1, blocking collectives, per_device(): paired = lax.all_gather(candidates, 'depth', axis=1, tiled=True)  8.97 us
    reduce_sum x1, other arithmetic, per_device(): ref_sq = jnp.sum(jnp.square(ref_whole.astype(jnp.float32)), axis=1)  2.07 us
  transfers between devices with their start and end apart: 2, of which 2 were waited for; matrix products, arithmetic and copies ran while one was open for 3% of the time, Pallas kernels for 0%

commit v1 on v0

--- a/solution.py
+++ b/solution.py
@@ -6,7 +6,12 @@
 
 def per_device(candidates, references, rates):
     paired = lax.all_gather(candidates, "depth", axis=1, tiled=True)
-    panel = lax.all_gather(paired, "col", axis=1, tiled=True)
+    ring = [paired]
+    for hop in range(3):
+        ring.append(lax.ppermute(ring[-1], "col", [(dev, (dev + 1) % 4) for dev in range(4)]))
+    panel = jnp.roll(
+        jnp.concatenate(ring[::-1], axis=1), (lax.axis_index("col") + 1) * ring[0].shape[1], axis=1
+    )
     width = panel.shape[1]
     cand_sq = jnp.sum(jnp.square(panel.astype(jnp.float32)), axis=1)
     ref_whole = lax.all_gather(references, "row", axis=1, tiled=True)

time: 86.5 us -> 56.7 us (0.66)
  waiting for transfers between devices: 50.1 us -> 24.1 us
  matrix products: 9.5 us -> 6.42 us
  starting transfers between devices: 0.04 us -> 1.76 us
  blocking collectives: 8.97 us -> 7.39 us
  other arithmetic: 4.24 us -> 3.17 us
    all_gather x1 -> x0, waiting for transfers between devices: 26.9 us -> none  [per_device(): panel = lax.all_gather(paired, 'col', axis=1, tiled=True)]
    ppermute x0 -> x3, waiting for transfers between devices: none -> 23.4 us  [per_device(): lax.ppermute(ring[-1], 'col', [(dev, (dev + 1) % 4) for dev in range(4)])]
    all_gather x1, waiting for transfers between devices: 22.4 us -> 0.01 us  [per_device(): ref_whole = lax.all_gather(references, 'row', axis=1, tiled=True)]
    dot_general x1, matrix products: 9.5 us -> 6.42 us  [per_device(): lax.dot_general(panel, ref_whole, (((1,), (1,)), ((), ())), preferred_ele...]
    ppermute x0 -> x3, starting transfers between devices: none -> 1.76 us  [per_device(): lax.ppermute(ring[-1], 'col', [(dev, (dev + 1) % 4) for dev in range(4)])]
    all_gather x1, blocking collectives: 8.97 us -> 7.39 us  [per_device(): paired = lax.all_gather(candidates, 'depth', axis=1, tiled=True)]
    reduce_sum x1, other arithmetic: 1.47 us -> 0.25 us  [per_device(): cand_sq = jnp.sum(jnp.square(panel.astype(jnp.float32)), axis=1)]
  transfers between devices with their start and end apart: 2 -> 4, of which waited for: 2 -> 3; matrix products, arithmetic and copies ran while one was open for 3% -> 2% of each run, Pallas kernels for 0% -> 0%
where the time goes in v1:
time: 56.7 us; the launch traced here: 56.5 us
  waiting for transfers between devices  24.1 us (43%)
  between operations  13.5 us (24%)
  blocking collectives  7.39 us (13%)
  matrix products  6.42 us (11%)
  other arithmetic  3.17 us (6%)
  starting transfers between devices  1.76 us (3%)
    ppermute x3, waiting for transfers between devices, per_device(): lax.ppermute(ring[-1], 'col', [(dev, (dev + 1) % 4) for dev in range(4)])  23.4 us
    all_gather x1, blocking collectives, per_device(): paired = lax.all_gather(candidates, 'depth', axis=1, tiled=True)  7.39 us
    dot_general x1, matrix products, per_device(): lax.dot_general(panel, ref_whole, (((1,), (1,)), ((), ())), preferred_ele...  6.42 us
    reduce_sum x1, other arithmetic, per_device(): ref_sq = jnp.sum(jnp.square(ref_whole.astype(jnp.float32)), axis=1)  2.22 us
    ppermute x3, starting transfers between devices, per_device(): lax.ppermute(ring[-1], 'col', [(dev, (dev + 1) % 4) for dev in range(4)])  1.76 us
  transfers between devices with their start and end apart: 4, of which 3 were waited for; matrix products, arithmetic and copies ran while one was open for 2% of the time, Pallas kernels for 0%

profile of v1, /device:TPU:0, one launch (start us, length us, event | category | flops | bytes accessed | tf_op | source)
XLA Modules:
  0.0 56.5 jit_solution(5615000896357319532)
XLA Ops:
  6.5 0.0 all-gather.2.cloned.1.call-start
  6.5 0.7 %all-gather.2.cloned.1.call-update = ((bf16[2048,128]{1,0:T(8,128)(2,1)}), bf16[2048,512]{1,0:T(8,128)(2,1)}) async-update(((), (), s32[]{:S(2)}) %all-gather.2.cloned.1.call-start, bf16[2048,128]{1,0:T(8,128)(2,1)} %param.4) | async-update | bytes 3145752
  7.3 7.4 %all_gather.6 = bf16[1024,128]{0,1:T(8,128)(2,1)S(1)} all-gather(bf16[1024,64]{0,1:T(8,128)(2,1)} %param.3), channel_id=1, replica_groups=mesh['row'=4,'col'=4,'depth'=2] {'depth'}, dimensions={1}, use_global_device_ids=true | all-gather | bytes 393216 | tf_op jit(solution)/shard_map/all_gather | solution.py:8
  14.6 1.8 %collective-permute-start = (bf16[1024,128]{0,1:T(8,128)(2,1)S(1)}, bf16[1024,128]{0,1:T(8,128)(2,1)S(1)}, u32[]{:S(2)}, u32[]{:S(2)}) collective-permute-start(bf16[1024,128]{0,1:T(8,128)(2,1)S(1)} %all_gather.6), channel_id=1, source_target_pairs={{0,2},{2,4},{4,6},{6,0},{1,3},{3,5},{5,7},{7,1},{8,10},{10,12},{12... | collective-permute-start | bytes 786440 | tf_op jit(solution)/shard_map/ppermute | solution.py:11
  16.4 7.5 %collective-permute-done = bf16[1024,128]{0,1:T(8,128)(2,1)S(1)} collective-permute-done((bf16[1024,128]{0,1:T(8,128)(2,1)S(1)}, bf16[1024,128]{0,1:T(8,128)(2,1)S(1)}, u32[]{:S(2)}, u32[]{:S(2)}) %collective-permute-start) | collective-permute-done | bytes 262176 | tf_op jit(solution)/shard_map/ppermute | solution.py:11
  23.9 0.0 collective-permute-start.1
  23.9 8.4 %collective-permute-done.1 = bf16[1024,128]{0,1:T(8,128)(2,1)S(1)} collective-permute-done((bf16[1024,128]{0,1:T(8,128)(2,1)S(1)}, bf16[1024,128]{0,1:T(8,128)(2,1)S(1)}, u32[]{:S(2)}, u32[]{:S(2)}) %collective-permute-start.1) | collective-permute-done | bytes 262176 | tf_op jit(solution)/shard_map/ppermute | solution.py:11
  32.3 0.0 collective-permute-start.2
  32.3 0.7 %neg.4 = f32[2048]{0:T(1024)S(1)} negate(f32[2048]{0:T(1024)} %param.5) | non-fusion elementwise | flops 2048 | bytes 16384 | tf_op jit(solution)/shard_map/neg | solution.py:23
  33.0 7.5 %collective-permute-done.2 = bf16[1024,128]{0,1:T(8,128)(2,1)S(1)} collective-permute-done((bf16[1024,128]{0,1:T(8,128)(2,1)S(1)}, bf16[1024,128]{0,1:T(8,128)(2,1)S(1)}, u32[]{:S(2)}, u32[]{:S(2)}) %collective-permute-start.2) | collective-permute-done | bytes 262176 | tf_op jit(solution)/shard_map/ppermute | solution.py:11
  40.7 0.3 multiply_reduce_fusion.1
  40.9 0.0 all-gather.2.cloned.1.call-done
  41.0 0.0 copy-start
  41.0 2.2 %multiply_reduce_fusion = f32[2048]{0:T(1024)S(1)} fusion(bf16[2048,512]{1,0:T(8,128)(2,1)} %all-gather.2.cloned.1.call-done), kind=kLoop, calls=%fused_computation.1 | loop fusion | flops 3143680 | bytes 2105344 | tf_op jit(solution)/shard_map/reduce_sum | solution.py:21
  43.2 0.0 copy-done
  43.2 6.4 %multiply_exponential_fusion = f32[1024,2048]{1,0:T(8,128)} fusion(bf16[2048,512]{1,0:T(8,128)(2,1)S(1)} %copy-done, f32[2048]{0:T(1024)S(1)} %multiply_reduce_fusion, f32[1024]{0:T(1024)S(1)} %multiply_reduce_fusion.1, f32[2048]{0:T(1024)S(1)} %neg.4, bf16[1024,1024]{0,1:T(8,128)(2,1)S(1)} %constant_dynamic-update-slice_fusion, s32[]{:T(128)S(6)} %select_n.14), kind=kOutput, calls=%fused_computation | convolution fusion | flops 2157969408 | bytes 11554820 | tf_op jit(solution)/shard_map/dot_general | solution.py:18
  (8 shorter events, 0.2 us)
Async XLA Ops:
  6.5 34.4 %all-gather.2.cloned.1.call-start = ((), (), s32[]{:S(2)}) async-start(), calls=%async_computation | async-start | bytes 2621440 | tf_op jit(solution)/shard_map/all_gather | solution.py:17
  14.6 9.3 %collective-permute-start = (bf16[1024,128]{0,1:T(8,128)(2,1)S(1)}, bf16[1024,128]{0,1:T(8,128)(2,1)S(1)}, u32[]{:S(2)}, u32[]{:S(2)}) collective-permute-start(bf16[1024,128]{0,1:T(8,128)(2,1)S(1)} %all_gather.6), channel_id=1, source_target_pairs={{0,2},{2,4},{4,6},{6,0},{1,3},{3,5},{5,7},{7,1},{8,10},{10,12},{12... | collective-permute-start | bytes 786440 | tf_op jit(solution)/shard_map/ppermute | solution.py:11
  23.9 8.4 %collective-permute-start.1 = (bf16[1024,128]{0,1:T(8,128)(2,1)S(1)}, bf16[1024,128]{0,1:T(8,128)(2,1)S(1)}, u32[]{:S(2)}, u32[]{:S(2)}) collective-permute-start(bf16[1024,128]{0,1:T(8,128)(2,1)S(1)} %collective-permute-done), channel_id=1, source_target_pairs={{0,2},{2,4},{4,6},{6,0},{1,3},{3,5},{5,7},{7,1},{8,10},{10,12},{12... | collective-permute-start | bytes 786440 | tf_op jit(solution)/shard_map/ppermute | solution.py:11
  32.3 8.2 %collective-permute-start.2 = (bf16[1024,128]{0,1:T(8,128)(2,1)S(1)}, bf16[1024,128]{0,1:T(8,128)(2,1)S(1)}, u32[]{:S(2)}, u32[]{:S(2)}) collective-permute-start(bf16[1024,128]{0,1:T(8,128)(2,1)S(1)} %collective-permute-done.1), channel_id=1, source_target_pairs={{0,2},{2,4},{4,6},{6,0},{1,3},{3,5},{5,7},{7,1},{8,10},{10,12},{12... | collective-permute-start | bytes 786440 | tf_op jit(solution)/shard_map/ppermute | solution.py:11
  41.0 2.2 %copy-start = (bf16[2048,512]{1,0:T(8,128)(2,1)S(1)}, bf16[2048,512]{1,0:T(8,128)(2,1)}, u32[]{:S(2)}) copy-start(bf16[2048,512]{1,0:T(8,128)(2,1)} %all-gather.2.cloned.1.call-done) | copy-start | bytes 6291460
Sparse Core Ops, SparseCore 0:
  8.9 25.5 all-gather.1
